TPU v7x, 32 devices: a whole 2x2x4 slice. The times are simulated.
32 devices in a mesh: elem: 8 (over z, y), dir: 4 (over x, core).
Axes of the slice: x: 2, y: 2, z: 4, core: 2. Of those that a mesh axis runs over, the one named last changes fastest.
Arguments:
- history: bfloat16 [8, 32, 3072], P(None, 'dir', 'elem'), may hold values from -6 to 6
- incident: bfloat16 [2, 32, 3072], P(None, 'dir', 'elem'), may hold values from -6 to 6
- ztiles: bfloat16 [24, 32, 128, 128], P('elem'), may hold values from -0.09375 to 0.09375
- zinv: bfloat16 [24, 128, 128], P('elem'), may hold values from -0.5 to 0.5
- columns: int32 [24, 32], P('elem'), may hold values from 0 to 23, as said below
- lags: int32 [24, 32], P('elem'), may hold values from 1 to 8
- counts: int32 [24], P('elem'), may hold values from 8 to 32
- basis: bfloat16 [3072, 256], P('elem'), may hold values from -0.15625 to 0.15625
Outputs:
- densities: bfloat16 [2, 32, 3072], P(None, 'dir', 'elem')
- far_field: float32 [2, 32, 256], P(None, 'dir', 'elem')
Inputs may be any that keep to these rules, and one draw needn't show every extreme that they name: A block row's slots at or beyond counts are unused; a source block may repeat within a row. `columns`: all slots, used or not, of the block rows of one index of elem name blocks whose panels lie on any one index of elem at most 12 times, and exactly 12 times for some index.
All inputs are finite; a program needn't handle non-finite values.
Results may differ from a plain program's by a relative error of at most 0.005.
Values may be sent and summed in bfloat16 or wider, within the bound.
A program may use at most 64 MiB of HBM per device.

v0:
```python
import jax
import jax.numpy as jnp
from jax import lax
from jax.sharding import PartitionSpec as P

STEPS = 2


def tile_product(picked, ztiles, counts):
    slot_index = jnp.arange(ztiles.shape[1], dtype=jnp.int32)
    active = slot_index[None, :] < counts[:, None]
    picked = jnp.where(active[:, :, None, None], picked, jnp.zeros((), picked.dtype))
    return jnp.einsum("rkdj,rkji->dri", picked, ztiles, preferred_element_type=jnp.float32)


def lagged_sum(gathered, ztiles, columns, lags, counts):
    levels, dir_count, panels = gathered.shape
    tile_size = ztiles.shape[2]
    grid = gathered.reshape(levels, dir_count, panels // tile_size, tile_size)
    picked = grid[lags - 1, :, columns, :]
    return tile_product(picked, ztiles, counts)


def finish_step(history_sum, own_field, zinv):
    dir_count, rows_block, tile_size = history_sum.shape
    own = own_field.astype(jnp.float32).reshape(dir_count, rows_block, tile_size)
    source = (own - history_sum).astype(jnp.bfloat16)
    density = jnp.einsum("drj,rji->dri", source, zinv, preferred_element_type=jnp.float32)
    return density.reshape(dir_count, rows_block * tile_size).astype(jnp.bfloat16)


def march_step(gathered, own_field, ztiles, zinv, columns, lags, counts):
    history_sum = lagged_sum(gathered, ztiles, columns, lags, counts)
    return finish_step(history_sum, own_field, zinv)


def on_device(history, incident, ztiles, zinv, columns, lags, counts, basis):
    dens_list = []
    far_list = []
    window = history
    for step_index in range(STEPS):
        gathered = lax.all_gather(window, "elem", axis=2, tiled=True)
        density = march_step(gathered, incident[step_index], ztiles, zinv, columns, lags, counts)
        dens_list.append(density)
        far_list.append(jnp.dot(density, basis, preferred_element_type=jnp.float32))
        window = jnp.concatenate([density[None], window[:-1]], axis=0)
    far_field = lax.psum_scatter(jnp.stack(far_list), "elem", scatter_dimension=2, tiled=True)
    return (jnp.stack(dens_list), far_field)


def solution(mesh):
    in_specs = (
        P(None, "dir", "elem"),
        P(None, "dir", "elem"),
        P("elem", None, None, None),
        P("elem", None, None),
        P("elem", None),
        P("elem", None),
        P("elem"),
        P("elem", None),
    )
    out_specs = (P(None, "dir", "elem"), P(None, "dir", "elem"))
    return jax.shard_map(
        on_device, mesh=mesh, in_specs=in_specs, out_specs=out_specs, check_vma=False
    )
```

profile of v0, /device:TPU:0, one launch (start us, length us, event | category | flops | bytes accessed | tf_op | source)
XLA Modules:
  0.0 152.6 jit_solution(1632386385600989006)
XLA Ops:
  7.2 0.0 copy-start
  7.2 0.0 reduce-scatter.4.cloned.1.call-start
  7.2 33.2 %all_gather.6 = bf16[8,8,3072]{2,1,0:T(8,128)(2,1)S(1)} all-gather(bf16[8,8,384]{2,1,0:T(8,128)(2,1)} %param.8), channel_id=1, replica_groups=mesh['elem'=8,'dir'=4] {'elem'}, dimensions={2}, use_global_device_ids=true | all-gather | bytes 442368 | tf_op jit(solution)/shard_map/all_gather | solution.py:42
  40.5 0.7 fusion.26
  41.2 0.1 reshape.69
  41.3 0.7 iota_compare_fusion
  42.0 1.8 %gather_fusion = bf16[96,8,128]{2,1,0:T(8,128)(2,1)} fusion(bf16[8,8,24,128]{3,1,2,0:T(8,128)(2,1)S(1)} %bitcast.65, s32[96]{0:T(128)S(1)} %reshape.69), kind=kCustom, calls=%fused_computation | custom fusion | bytes 393984 | tf_op jit(solution)/shard_map/gather | solution.py:20
  43.8 0.0 slice-start
  43.8 0.0 copy-done
  43.8 1.7 %convolution_convert_fusion.1 = bf16[3,8,128]{2,1,0:T(8,128)(2,1)S(1)} fusion(bf16[3,128,128]{2,1,0:T(8,128)(2,1)} %param.11, bf16[3,32,128,128]{3,2,1,0:T(8,128)(2,1)S(1)} %copy-done, bf16[3,32,8,128]{3,2,1,0:T(8,128)(2,1)} %bitcast.68, pred[3,32]{1,0:T(4,128)(4,1)S(1)} %iota_compare_fusion, bf16[2,8,384]{2,1,0:T(8,128)(2,1)} %param.9), kind=kOutput, calls=%fused_computation.7 | convolution fusion | flops 26062848 | bytes 3453024 | tf_op jit(solution)/shard_map/drj,rji->dri/dot_general | solution.py:28
  45.5 0.0 slice-done
  45.5 31.0 %all_gather.7 = bf16[8,8,3072]{2,1,0:T(8,128)(2,1)S(1)} all-gather(bf16[8,8,384]{2,1,0:T(8,128)(2,1)S(1)} %pad_maximum_fusion), channel_id=1, replica_groups=mesh['elem'=8,'dir'=4] {'elem'}, dimensions={2}, use_global_device_ids=true | all-gather | bytes 442368 | tf_op jit(solution)/shard_map/all_gather | solution.py:42
  76.6 1.8 %gather_fusion.1 = bf16[96,8,128]{2,1,0:T(8,128)(2,1)} fusion(bf16[8,8,24,128]{3,1,2,0:T(8,128)(2,1)S(1)} %bitcast.66, s32[96]{0:T(128)S(1)} %reshape.69), kind=kCustom, calls=%fused_computation.1 | custom fusion | bytes 393984 | tf_op jit(solution)/shard_map/gather | solution.py:20
  78.4 1.7 %convolution_convert_fusion = bf16[3,8,128]{2,1,0:T(8,128)(2,1)S(1)} fusion(bf16[3,128,128]{2,1,0:T(8,128)(2,1)} %param.11, bf16[3,32,128,128]{3,2,1,0:T(8,128)(2,1)S(1)} %copy-done, bf16[3,32,8,128]{3,2,1,0:T(8,128)(2,1)} %bitcast.67, pred[3,32]{1,0:T(4,128)(4,1)S(1)} %iota_compare_fusion, bf16[2,8,384]{2,1,0:T(8,128)(2,1)} %param.9), kind=kOutput, calls=%fused_computation.6 | convolution fusion | flops 26062848 | bytes 3453024 | tf_op jit(solution)/shard_map/drj,rji->dri/dot_general | solution.py:28
  80.1 0.0 copy-done.1
  80.1 0.1 convolution_bitcast_fusion.3
  80.3 0.1 convolution_bitcast_fusion.2
  80.4 0.2 copy.12
  80.6 0.8 reshape.95
  81.5 0.0 reduce-scatter.4.cloned.1.call-update
  81.5 0.6 pad_maximum_fusion.2
  82.1 62.2 %reduce-scatter.4.cloned.1.call-done = f32[32,16]{1,0:T(8,128)} async-done(((f32[256,16]{1,0:T(8,128)}), f32[32,16]{1,0:T(8,128)}) %reduce-scatter.4.cloned.1.call-update) | async-done | bytes 2064
  144.3 0.8 reshape.96
  145.1 0.7 copy.13
  (3 shorter events, 0.0 us)
Async XLA Ops:
  7.2 36.6 %copy-start = (bf16[3,32,128,128]{3,2,1,0:T(8,128)(2,1)S(1)}, bf16[3,32,128,128]{3,2,1,0:T(8,128)(2,1)}, u32[]{:S(2)}) copy-start(bf16[3,32,128,128]{3,2,1,0:T(8,128)(2,1)} %param.10) | copy-start | bytes 9437188
  7.2 137.1 %reduce-scatter.4.cloned.1.call-start = ((), (), s32[]{:S(2)}) async-start(), calls=%async_computation.1 | async-start | bytes 147456
  43.8 1.7 %slice-start = ((bf16[8,8,384]{2,1,0:T(8,128)(2,1)}), bf16[7,8,384]{2,1,0:T(8,128)(2,1)S(1)}, s32[]{:S(2)}) async-start(bf16[8,8,384]{2,1,0:T(8,128)(2,1)} %param.8), calls=%async_computation.2 | async-start | bytes 86016 | tf_op jit(solution)/shard_map/slice | solution.py:46
  78.4 1.7 %copy-start.1 = (bf16[384,256]{1,0:T(8,128)(2,1)S(1)}, bf16[384,256]{1,0:T(8,128)(2,1)}, u32[]{:S(2)}) copy-start(bf16[384,256]{1,0:T(8,128)(2,1)} %param.15) | copy-start | bytes 589828
Sparse Core Ops, SparseCore 0:
  81.6 62.6 reduce-scatter.3
where the time goes:
time: 153 us
  blocking collectives  64.3 us (42%)
  waiting for transfers between devices  62.2 us (41%)
  between operations  14.1 us (9%)
  local copies, waits for them, and re-layouts  6.24 us (4%)
  matrix products  3.71 us (2%)
  other arithmetic  2.07 us (1%)
    all_gather x2, blocking collectives, on_device(): gathered = lax.all_gather(window, 'elem', axis=2, tiled=True)  64.3 us
    unnamed x2, waiting for transfers between devices  62.2 us
    gather x2, local copies, waits for them, and re-layouts, lagged_sum(): picked = grid[lags - 1, :, columns, :]  3.64 us
    dot_general x2, matrix products, finish_step(): jnp.einsum('drj,rji->dri', source, zinv, preferred_element_type=jnp.float32)  3.42 us
  transfers between devices with their start and end apart: 1, of which 1 were waited for; matrix products, arithmetic and copies ran while one was open for 0% of the time, Pallas kernels for 0%

commit v1 on v0

v1 whole, which is shorter than its diff:
```python
import functools

import jax
import jax.numpy as jnp
from jax import lax
from jax.experimental import pallas as pl
from jax.experimental.pallas import tpu as pltpu
from jax.sharding import PartitionSpec as P

MESH = pl.DeviceIdType.MESH
LANES = 128


def march_kernel(n, hist_hbm, inc_hbm, z_hbm, zinv_hbm, basis_hbm, where_from,
                 dens_out, far_out,
                 ext, ztile, zinv, basis, inc, picked, picked1, dens0, part, far_in,
                 load_sem, own_sem, hist_send, hist_recv, relay_send, dens_send, dens_recv,
                 far_send, far_recv):
    me = lax.axis_index("elem")
    _, rows, slots = where_from.shape
    levels, dirs, width = hist_hbm.shape
    half = n // 2
    partner = me + 1 - 2 * lax.rem(me, 2)
    owned = far_out.shape[2]

    per = levels * rows
    own_copies = [
        pltpu.make_async_copy(
            hist_hbm.at[level, :, pl.ds(row * LANES, LANES)],
            ext.at[me * per + level * rows + row], own_sem.at[level * rows + row])
        for level in range(levels) for row in range(rows)]
    for copy in own_copies:
        copy.start()
    loads = [
        pltpu.make_async_copy(z_hbm, ztile, load_sem.at[1]),
        pltpu.make_async_copy(zinv_hbm, zinv, load_sem.at[2]),
        pltpu.make_async_copy(basis_hbm, basis, load_sem.at[3]),
        pltpu.make_async_copy(inc_hbm, inc, load_sem.at[4]),
    ]
    barrier = pltpu.get_barrier_semaphore()
    for off in range(1, n):
        pl.semaphore_signal(barrier, inc=1, device_id={"elem": lax.rem(me + off, n)},
                            device_id_type=MESH)
    for load in loads:
        load.start()
    for copy in own_copies:
        copy.wait()
    pl.semaphore_wait(barrier, n - 1)

    def send_block(block, target, sem):
        return pltpu.make_async_remote_copy(
            src_ref=ext.at[pl.ds(block * per, per)],
            dst_ref=ext.at[pl.ds(block * per, per)],
            send_sem=sem, recv_sem=hist_recv.at[block],
            device_id={"elem": target}, device_id_type=MESH)

    sends = [send_block(me, partner, hist_send.at[0])]
    for off in range(1, half):
        sends.append(send_block(me, lax.rem(me + 2 * off, n), hist_send.at[off]))
    for copy in sends:
        copy.start()

    ext[n * per] = jnp.zeros((dirs, LANES), ext.dtype)
    dens0[n * rows] = jnp.zeros((dirs, LANES), dens0.dtype)

    relays = []
    for off in range(1, half):
        block = lax.rem(me + n - 2 * off, n)
        send_block(block, partner, relay_send.at[off]).wait_recv()
        relay = send_block(block, partner, relay_send.at[off])
        relay.start()
        relays.append(relay)
    send_block(partner, partner, relay_send.at[0]).wait_recv()
    for off in range(1, half):
        block = lax.rem(partner + n - 2 * off, n)
        send_block(block, partner, relay_send.at[off]).wait_recv()
    for copy in sends + relays:
        copy.wait_send()
    for load in loads:
        load.wait()

    sums = []
    for row in range(rows):
        for slot in range(slots):
            lanes = pl.ds(slot * LANES, LANES)
            picked[row, 0:dirs, lanes] = ext[where_from[0, row, slot]]
            picked[row, dirs:2 * dirs, lanes] = ext[where_from[1, row, slot]]
        sums.append(jnp.dot(picked[row], ztile[row], preferred_element_type=jnp.float32))

    def density_of(step, row, history_sum):
        own = inc[step, :, row * LANES:(row + 1) * LANES].astype(jnp.float32)
        source = (own - history_sum).astype(jnp.bfloat16)
        return jnp.dot(source, zinv[row], preferred_element_type=jnp.float32).astype(jnp.bfloat16)

    for row in range(rows):
        density = density_of(0, row, sums[row][0:dirs])
        dens0[me * rows + row] = density
        dens_out[0, :, row * LANES:(row + 1) * LANES] = density

    def send_density(off):
        return pltpu.make_async_remote_copy(
            src_ref=dens0.at[pl.ds(me * rows, rows)], dst_ref=dens0.at[pl.ds(me * rows, rows)],
            send_sem=dens_send.at[off], recv_sem=dens_recv.at[off],
            device_id={"elem": lax.rem(me + off, n)}, device_id_type=MESH)

    dens_copies = [send_density(off) for off in range(1, n)]
    for copy in dens_copies:
        copy.start()

    def far_copies(step):
        copies = []
        for off in range(1, n):
            target = lax.rem(me + off, n)
            tile = target * owned // LANES
            copies.append(pltpu.make_async_remote_copy(
                src_ref=part.at[step, tile], dst_ref=far_in.at[step, off],
                send_sem=far_send.at[step, off], recv_sem=far_recv.at[step, off],
                device_id={"elem": target}, device_id_type=MESH))
        return copies

    def far_parts(step, density):
        value = jnp.dot(density, basis[...], preferred_element_type=jnp.float32)
        for tile in range(part.shape[1]):
            part[step, tile] = value[:, tile * LANES:(tile + 1) * LANES]

    far_parts(0, dens_out[0])
    far0 = far_copies(0)
    for copy in far0:
        copy.start()

    for copy in dens_copies:
        copy.wait()
    for row in range(rows):
        for slot in range(slots):
            picked1[row, :, pl.ds(slot * LANES, LANES)] = dens0[where_from[2, row, slot]]
        total = sums[row][dirs:2 * dirs] + jnp.dot(
            picked1[row], ztile[row], preferred_element_type=jnp.float32)
        dens_out[1, :, row * LANES:(row + 1) * LANES] = density_of(1, row, total)
    far_parts(1, dens_out[1])
    far1 = far_copies(1)
    for copy in far1:
        copy.start()
    shift = lax.rem(me * owned, LANES)
    for step, copies in ((0, far0), (1, far1)):
        for copy in copies:
            copy.wait()
        total = part[step, me * owned // LANES]
        for off in range(1, n):
            total = total + far_in[step, off]
        total = pltpu.roll(total, lax.rem(LANES - shift, LANES), 1)
        far_out[step] = total[:, 0:owned]


def on_device(history, incident, ztiles, zinv, columns, lags, counts, basis, *, n):
    steps, dirs, width = incident.shape
    levels = history.shape[0]
    rows, slots, tile, _ = ztiles.shape
    coeffs = basis.shape[1]
    flat = ztiles.reshape(rows, slots * tile, tile)
    active = jnp.arange(slots, dtype=jnp.int32)[None, :] < counts[:, None]
    kind = jnp.arange(3, dtype=jnp.int32)[:, None, None]
    back = lags[None] - 1 - kind
    in_history = ((columns // rows)[None] * levels + back) * rows + (columns % rows)[None]
    where_from = jnp.where(
        kind < 2,
        jnp.where(active[None] & (back >= 0), in_history, n * levels * rows),
        jnp.where(active & (lags == 1), columns, n * rows)[None])
    any_spec = pl.BlockSpec(memory_space=pl.ANY)
    smem = pl.BlockSpec(memory_space=pltpu.SMEM)
    vmem = pl.BlockSpec(memory_space=pltpu.VMEM)
    bf16, f32 = jnp.bfloat16, jnp.float32
    dma = pltpu.SemaphoreType.DMA
    tiles = coeffs // LANES
    return pl.pallas_call(
        functools.partial(march_kernel, n),
        out_shape=(jax.ShapeDtypeStruct((steps, dirs, width), bf16),
                   jax.ShapeDtypeStruct((steps, dirs, coeffs // n), f32)),
        in_specs=[any_spec] * 5 + [smem],
        out_specs=(vmem, vmem),
        scratch_shapes=[
            pltpu.VMEM((n * levels * rows + 1, dirs, LANES), bf16),
            pltpu.VMEM(flat.shape, bf16),
            pltpu.VMEM(zinv.shape, bf16),
            pltpu.VMEM(basis.shape, bf16),
            pltpu.VMEM(incident.shape, bf16),
            pltpu.VMEM((rows, 2 * dirs, slots * tile), bf16),
            pltpu.VMEM((rows, dirs, slots * tile), bf16),
            pltpu.VMEM((n * rows + 1, dirs, LANES), bf16),
            pltpu.VMEM((steps, tiles, dirs, LANES), f32),
            pltpu.VMEM((steps, n, dirs, LANES), f32),
            dma((5,)), dma((levels * rows,)),
            dma((n,)), dma((n,)), dma((n,)),
            dma((n,)), dma((n,)),
            dma((steps, n)), dma((steps, n)),
        ],
        compiler_params=pltpu.CompilerParams(
            collective_id=0, has_side_effects=True, vmem_limit_bytes=48 * 1024 * 1024),
    )(history, incident, flat, zinv, basis, where_from)


def solution(mesh):
    in_specs = (
        P(None, "dir", "elem"),
        P(None, "dir", "elem"),
        P("elem", None, None, None),
        P("elem", None, None),
        P("elem", None),
        P("elem", None),
        P("elem"),
        P("elem", None),
    )
    out_specs = (P(None, "dir", "elem"), P(None, "dir", "elem"))
    return jax.shard_map(
        functools.partial(on_device, n=mesh.shape["elem"]), mesh=mesh,
        in_specs=in_specs, out_specs=out_specs, check_vma=False)
```

time: 153 us -> 34.7 us (0.23)
  blocking collectives: 64.3 us -> 0 us
  waiting for transfers between devices: 62.2 us -> 0 us
  Pallas kernels: 0 us -> 25.7 us
  between operations: 14.1 us -> 0.64 us
  matrix products: 3.71 us -> 0 us
    all_gather x2 -> x0, blocking collectives: 64.3 us -> none  [on_device(): gathered = lax.all_gather(window, 'elem', axis=2, tiled=True)]
    unnamed x2 -> x0, waiting for transfers between devices: 62.2 us -> none
    pallas_call x0 -> x1, Pallas kernels: none -> 25.7 us  [on_device(): pl.pallas_call(functools.partial(march_kernel, n), out_shape=(jax.ShapeDt...]
    unnamed x8 -> x12, local copies, waits for them, and re-layouts: 2.51 us -> 6.41 us
    dot_general x4 -> x0, matrix products: 3.71 us -> none  [the longest x2 3.42 us: finish_step(): jnp.einsum('drj,rji->dri', source, zinv, preferred_element_type=jnp.float32)]
    gather x2 -> x0, local copies, waits for them, and re-layouts: 3.64 us -> none  [lagged_sum(): picked = grid[lags - 1, :, columns, :]]
  transfers between devices with their start and end apart: 1 -> 0, of which waited for: 1 -> 0; matrix products, arithmetic and copies ran while one was open for 0% -> 0% of each run, Pallas kernels for 0% -> 0%
where the time goes in v1:
time: 34.7 us; the launch traced here: 34.3 us
  Pallas kernels  25.7 us (74%)
  local copies, waits for them, and re-layouts  6.41 us (18%)
  other arithmetic  1.58 us (5%)
  between operations  0.64 us (2%)
    pallas_call x1, Pallas kernels, on_device(): pl.pallas_call(functools.partial(march_kernel, n), out_shape=(jax.ShapeDt...  25.7 us
    unnamed x12, local copies, waits for them, and re-layouts  6.41 us
    sub x1, other arithmetic, on_device(): back = lags[None] - 1 - kind  0.77 us
    lt x1, other arithmetic, on_device(): active = jnp.arange(slots, dtype=jnp.int32)[None, :] < counts[:, None]  0.73 us

profile of v1, /device:TPU:0, one launch (start us, length us, event | category | flops | bytes accessed | tf_op | source)
XLA Modules:
  0.0 34.3 jit_solution(6268632576526473528)
XLA Ops:
  0.6 0.7 %iota_compare_fusion = pred[3,32]{1,0:T(4,128)(4,1)S(1)} fusion(s32[3]{0:T(128)} %param.14), kind=kLoop, calls=%fused_computation.7 | loop fusion | flops 96 | bytes 108 | tf_op jit(solution)/shard_map/lt | solution.py:160
  1.4 0.8 %broadcast_add_fusion = (s32[3,32]{1,0:T(4,128)S(1)}, s32[3,32]{1,0:T(4,128)S(1)}, s32[3,32]{1,0:T(4,128)S(1)}, s32[3,32]{1,0:T(4,128)S(1)}) fusion(s32[3,32]{1,0:T(4,128)} %param.13, s32[3,32]{1,0:T(4,128)} %param.12, s32[3]{0:T(128)} %param.14), kind=kLoop, calls=%fused_computation.12 | loop fusion | flops 1728 | bytes 2316 | tf_op jit(solution)/shard_map/sub | solution.py:162
  2.1 0.1 select_select_fusion.where_from
  2.2 0.0 copy-start
  2.2 1.9 %copy-done = bf16[3,32,128,128]{3,2,1,0:T(8,128)(2,1)S(1)} copy-done((bf16[3,32,128,128]{3,2,1,0:T(8,128)(2,1)S(1)}, bf16[3,32,128,128]{3,2,1,0:T(8,128)(2,1)}, u32[]{:S(2)}) %copy-start) | copy-done | bytes 3145752
  4.1 0.0 copy-start.1
  4.1 0.9 %copy-done.1 = bf16[384,256]{1,0:T(8,128)(2,1)S(1)} copy-done((bf16[384,256]{1,0:T(8,128)(2,1)S(1)}, bf16[384,256]{1,0:T(8,128)(2,1)}, u32[]{:S(2)}) %copy-start.1) | copy-done | bytes 196632
  5.0 0.0 copy-start.2
  5.0 0.9 %copy-done.2 = bf16[3,128,128]{2,1,0:T(8,128)(2,1)S(1)} copy-done((bf16[3,128,128]{2,1,0:T(8,128)(2,1)S(1)}, bf16[3,128,128]{2,1,0:T(8,128)(2,1)}, u32[]{:S(2)}) %copy-start.2) | copy-done | bytes 98328
  5.9 0.0 copy-start.3
  5.9 0.8 %copy-done.3 = bf16[8,8,384]{2,1,0:T(8,128)(2,1)S(1)} copy-done((bf16[8,8,384]{2,1,0:T(8,128)(2,1)S(1)}, bf16[8,8,384]{2,1,0:T(8,128)(2,1)}, u32[]{:S(2)}) %copy-start.3) | copy-done | bytes 49176
  6.7 0.0 copy-start.4
  6.7 0.7 %copy-done.4 = bf16[2,8,384]{2,1,0:T(8,128)(2,1)S(1)} copy-done((bf16[2,8,384]{2,1,0:T(8,128)(2,1)S(1)}, bf16[2,8,384]{2,1,0:T(8,128)(2,1)}, u32[]{:S(2)}) %copy-start.4) | copy-done | bytes 12312
  7.4 25.7 %shard_map.95 = (bf16[2,8,384]{2,1,0:T(8,128)(2,1)S(1)}, f32[2,8,32]{2,1,0:T(8,128)S(1)}) custom-call(bf16[8,8,384]{2,1,0:T(8,128)(2,1)S(1)} %copy-done.3, bf16[2,8,384]{2,1,0:T(8,128)(2,1)S(1)} %copy-done.4, bf16[3,4096,128]{2,1,0:T(8,128)(2,1)S(1)} %bitcast.1, bf16[3,128,128]{2,1,0:T(8,128)(2,1)S(1)} %copy-done.2, bf16[384,256]{1,0:T(8,128)(2,1)S(1)} %copy-done.1, ...), custom_call_target="tpu_custom_call" | custom-call | tf_op jit(solution)/shard_map/pallas_call | solution.py:174
  33.1 0.6 %copy.12 = bf16[2,8,384]{2,1,0:T(8,128)(2,1)} copy(bf16[2,8,384]{2,1,0:T(8,128)(2,1)S(1)} %get-tuple-element.8) | data formatting | bytes 24576
  33.7 0.6 %copy.13 = f32[2,8,32]{2,1,0:T(8,128)} copy(f32[2,8,32]{2,1,0:T(8,128)S(1)} %get-tuple-element.9) | data formatting | bytes 4096
  (1 shorter events, 0.0 us)
Async XLA Ops:
  2.2 1.9 %copy-start = (bf16[3,32,128,128]{3,2,1,0:T(8,128)(2,1)S(1)}, bf16[3,32,128,128]{3,2,1,0:T(8,128)(2,1)}, u32[]{:S(2)}) copy-start(bf16[3,32,128,128]{3,2,1,0:T(8,128)(2,1)} %param.10) | copy-start | bytes 9437188
  4.1 0.9 %copy-start.1 = (bf16[384,256]{1,0:T(8,128)(2,1)S(1)}, bf16[384,256]{1,0:T(8,128)(2,1)}, u32[]{:S(2)}) copy-start(bf16[384,256]{1,0:T(8,128)(2,1)} %basis_hbm.1) | copy-start | bytes 589828
  5.0 0.9 %copy-start.2 = (bf16[3,128,128]{2,1,0:T(8,128)(2,1)S(1)}, bf16[3,128,128]{2,1,0:T(8,128)(2,1)}, u32[]{:S(2)}) copy-start(bf16[3,128,128]{2,1,0:T(8,128)(2,1)} %zinv_hbm.1) | copy-start | bytes 294916
  5.9 0.8 %copy-start.3 = (bf16[8,8,384]{2,1,0:T(8,128)(2,1)S(1)}, bf16[8,8,384]{2,1,0:T(8,128)(2,1)}, u32[]{:S(2)}) copy-start(bf16[8,8,384]{2,1,0:T(8,128)(2,1)} %hist_hbm.1) | copy-start | bytes 147460
  6.7 0.7 %copy-start.4 = (bf16[2,8,384]{2,1,0:T(8,128)(2,1)S(1)}, bf16[2,8,384]{2,1,0:T(8,128)(2,1)}, u32[]{:S(2)}) copy-start(bf16[2,8,384]{2,1,0:T(8,128)(2,1)} %inc_hbm.1) | copy-start | bytes 36868

commit v2 on v1

--- a/solution.py
+++ b/solution.py
@@ -11,13 +11,13 @@
 LANES = 128
 
 
-def march_kernel(n, hist_hbm, inc_hbm, z_hbm, zinv_hbm, basis_hbm, where_from,
+def march_kernel(n, hist_hbm, inc_hbm, z_hbm, zinv_hbm, basis_hbm, cols, lags, counts,
                  dens_out, far_out,
                  ext, ztile, zinv, basis, inc, picked, picked1, dens0, part, far_in,
                  load_sem, own_sem, hist_send, hist_recv, relay_send, dens_send, dens_recv,
                  far_send, far_recv):
     me = lax.axis_index("elem")
-    _, rows, slots = where_from.shape
+    rows, slots = cols.shape
     levels, dirs, width = hist_hbm.shape
     half = n // 2
     partner = me + 1 - 2 * lax.rem(me, 2)
@@ -63,6 +63,18 @@
     ext[n * per] = jnp.zeros((dirs, LANES), ext.dtype)
     dens0[n * rows] = jnp.zeros((dirs, LANES), dens0.dtype)
 
+    from_hist0, from_hist1, from_dens = [], [], []
+    for row in range(rows):
+        live = counts[row]
+        for slot in range(slots):
+            column, lag = cols[row, slot], lags[row, slot]
+            lag = jnp.where(slot < live, lag, 0)
+            base = lax.div(column, rows) * per + lax.rem(column, rows) - rows
+            newest = base + lag * rows
+            from_hist0.append(jnp.where(lag > 0, newest, n * per))
+            from_hist1.append(jnp.where(lag > 1, newest - rows, n * per))
+            from_dens.append(jnp.where(lag == 1, column, n * rows))
+
     relays = []
     for off in range(1, half):
         block = lax.rem(me + n - 2 * off, n)
@@ -83,8 +95,8 @@
     for row in range(rows):
         for slot in range(slots):
             lanes = pl.ds(slot * LANES, LANES)
-            picked[row, 0:dirs, lanes] = ext[where_from[0, row, slot]]
-            picked[row, dirs:2 * dirs, lanes] = ext[where_from[1, row, slot]]
+            picked[row, 0:dirs, lanes] = ext[from_hist0[row * slots + slot]]
+            picked[row, dirs:2 * dirs, lanes] = ext[from_hist1[row * slots + slot]]
         sums.append(jnp.dot(picked[row], ztile[row], preferred_element_type=jnp.float32))
 
     def density_of(step, row, history_sum):
@@ -132,7 +144,7 @@
         copy.wait()
     for row in range(rows):
         for slot in range(slots):
-            picked1[row, :, pl.ds(slot * LANES, LANES)] = dens0[where_from[2, row, slot]]
+            picked1[row, :, pl.ds(slot * LANES, LANES)] = dens0[from_dens[row * slots + slot]]
         total = sums[row][dirs:2 * dirs] + jnp.dot(
             picked1[row], ztile[row], preferred_element_type=jnp.float32)
         dens_out[1, :, row * LANES:(row + 1) * LANES] = density_of(1, row, total)
@@ -157,15 +169,7 @@
     rows, slots, tile, _ = ztiles.shape
     coeffs = basis.shape[1]
     flat = ztiles.reshape(rows, slots * tile, tile)
-    active = jnp.arange(slots, dtype=jnp.int32)[None, :] < counts[:, None]
-    kind = jnp.arange(3, dtype=jnp.int32)[:, None, None]
-    back = lags[None] - 1 - kind
-    in_history = ((columns // rows)[None] * levels + back) * rows + (columns % rows)[None]
-    where_from = jnp.where(
-        kind < 2,
-        jnp.where(active[None] & (back >= 0), in_history, n * levels * rows),
-        jnp.where(active & (lags == 1), columns, n * rows)[None])
-    any_spec = pl.BlockSpec(memory_space=pl.ANY)
+    hbm = pl.BlockSpec(memory_space=pltpu.HBM)
     smem = pl.BlockSpec(memory_space=pltpu.SMEM)
     vmem = pl.BlockSpec(memory_space=pltpu.VMEM)
     bf16, f32 = jnp.bfloat16, jnp.float32
@@ -175,7 +179,7 @@
         functools.partial(march_kernel, n),
         out_shape=(jax.ShapeDtypeStruct((steps, dirs, width), bf16),
                    jax.ShapeDtypeStruct((steps, dirs, coeffs // n), f32)),
-        in_specs=[any_spec] * 5 + [smem],
+        in_specs=[hbm] * 5 + [smem] * 3,
         out_specs=(vmem, vmem),
         scratch_shapes=[
             pltpu.VMEM((n * levels * rows + 1, dirs, LANES), bf16),
@@ -194,8 +198,8 @@
             dma((steps, n)), dma((steps, n)),
         ],
         compiler_params=pltpu.CompilerParams(
-            collective_id=0, has_side_effects=True, vmem_limit_bytes=48 * 1024 * 1024),
-    )(history, incident, flat, zinv, basis, where_from)
+            collective_id=0, has_side_effects=True, vmem_limit_bytes=67043328),
+    )(history, incident, flat, zinv, basis, columns, lags, counts)
 
 
 def solution(mesh):

time: 34.7 us -> 29.9 us (0.86)
  local copies, waits for them, and re-layouts: 6.41 us -> 2.6 us
  other arithmetic: 1.58 us -> 0 us
  Pallas kernels: 25.7 us -> 26.3 us
    unnamed x12 -> x2, local copies, waits for them, and re-layouts: 6.41 us -> 2.6 us
    sub x1 -> x0, other arithmetic: 0.77 us -> none  [on_device(): back = lags[None] - 1 - kind]
    lt x2 -> x0, other arithmetic: 0.73 us -> none  [the longest x1 0.73 us: on_device(): active = jnp.arange(slots, dtype=jnp.int32)[None, :] < counts[:, None]]
    pallas_call x1, Pallas kernels: 25.7 us -> 26.3 us  [on_device(): pl.pallas_call(functools.partial(march_kernel, n), out_shape=(jax.ShapeDt...]
where the time goes in v2:
time: 29.9 us; the launch traced here: 29.6 us
  Pallas kernels  26.3 us (88%)
  local copies, waits for them, and re-layouts  2.6 us (9%)
  between operations  0.64 us (2%)
    pallas_call x1, Pallas kernels, on_device(): pl.pallas_call(functools.partial(march_kernel, n), out_shape=(jax.ShapeDt...  26.3 us
    unnamed x2, local copies, waits for them, and re-layouts  2.6 us

profile of v2, /device:TPU:0, one launch (start us, length us, event | category | flops | bytes accessed | tf_op | source)
XLA Modules:
  0.0 29.6 jit_solution(8912417830328387405)
XLA Ops:
  0.6 26.3 %shard_map.95 = (bf16[2,8,384]{2,1,0:T(8,128)(2,1)}, f32[2,8,32]{2,1,0:T(8,128)}) custom-call(bf16[8,8,384]{2,1,0:T(8,128)(2,1)} %hist_hbm.1, bf16[2,8,384]{2,1,0:T(8,128)(2,1)} %inc_hbm.1, bf16[3,4096,128]{2,1,0:T(8,128)(2,1)} %bitcast.1, bf16[3,128,128]{2,1,0:T(8,128)(2,1)} %zinv_hbm.1, bf16[384,256]{1,0:T(8,128)(2,1)} %basis_hbm.1, s32[3,32]{1,0:T(4,128)} %cols.1, ...), custom_call_target="tpu_custom_call" | custom-call | tf_op jit(solution)/shard_map/pallas_call | solution.py:178
  27.0 1.3 %copy.12 = bf16[2,8,384]{2,1,0:T(8,128)(2,1)} copy(bf16[2,8,384]{2,1,0:T(8,128)(2,1)} %get-tuple-element.4) | data formatting | bytes 24576
  28.3 1.3 %copy.13 = f32[2,8,32]{2,1,0:T(8,128)} copy(f32[2,8,32]{2,1,0:T(8,128)} %get-tuple-element.5) | data formatting | bytes 4096

commit v3 on v2

--- a/solution.py
+++ b/solution.py
@@ -11,9 +11,10 @@
 LANES = 128
 
 
-def march_kernel(n, hist_hbm, inc_hbm, z_hbm, zinv_hbm, basis_hbm, cols, lags, counts,
+def march_kernel(n, hist_hbm, inc_hbm, z_hbm, zinv_hbm, basis_hbm, cols_hbm,
+                 lags_hbm, counts_hbm,
                  dens_out, far_out,
-                 ext, ztile, zinv, basis, inc, picked, picked1, dens0, part, far_in,
+                 ext, ztile, zinv, basis, inc, cols, lags, counts, picked, picked1, dens0, part, far_in,
                  load_sem, own_sem, hist_send, hist_recv, relay_send, dens_send, dens_recv,
                  far_send, far_recv):
     me = lax.axis_index("elem")
@@ -31,6 +32,11 @@
         for level in range(levels) for row in range(rows)]
     for copy in own_copies:
         copy.start()
+    tables = [
+        pltpu.make_async_copy(cols_hbm, cols, load_sem.at[0]),
+        pltpu.make_async_copy(lags_hbm, lags, load_sem.at[5]),
+        pltpu.make_async_copy(counts_hbm, counts, load_sem.at[6]),
+    ]
     loads = [
         pltpu.make_async_copy(z_hbm, ztile, load_sem.at[1]),
         pltpu.make_async_copy(zinv_hbm, zinv, load_sem.at[2]),
@@ -41,28 +47,13 @@
     for off in range(1, n):
         pl.semaphore_signal(barrier, inc=1, device_id={"elem": lax.rem(me + off, n)},
                             device_id_type=MESH)
-    for load in loads:
+    for load in tables + loads:
         load.start()
-    for copy in own_copies:
-        copy.wait()
-    pl.semaphore_wait(barrier, n - 1)
-
-    def send_block(block, target, sem):
-        return pltpu.make_async_remote_copy(
-            src_ref=ext.at[pl.ds(block * per, per)],
-            dst_ref=ext.at[pl.ds(block * per, per)],
-            send_sem=sem, recv_sem=hist_recv.at[block],
-            device_id={"elem": target}, device_id_type=MESH)
-
-    sends = [send_block(me, partner, hist_send.at[0])]
-    for off in range(1, half):
-        sends.append(send_block(me, lax.rem(me + 2 * off, n), hist_send.at[off]))
-    for copy in sends:
-        copy.start()
-
     ext[n * per] = jnp.zeros((dirs, LANES), ext.dtype)
     dens0[n * rows] = jnp.zeros((dirs, LANES), dens0.dtype)
 
+    for load in tables:
+        load.wait()
     from_hist0, from_hist1, from_dens = [], [], []
     for row in range(rows):
         live = counts[row]
@@ -74,6 +65,23 @@
             from_hist0.append(jnp.where(lag > 0, newest, n * per))
             from_hist1.append(jnp.where(lag > 1, newest - rows, n * per))
             from_dens.append(jnp.where(lag == 1, column, n * rows))
+
+    for copy in own_copies:
+        copy.wait()
+    pl.semaphore_wait(barrier, n - 1)
+
+    def send_block(block, target, sem):
+        return pltpu.make_async_remote_copy(
+            src_ref=ext.at[pl.ds(block * per, per)],
+            dst_ref=ext.at[pl.ds(block * per, per)],
+            send_sem=sem, recv_sem=hist_recv.at[block],
+            device_id={"elem": target}, device_id_type=MESH)
+
+    sends = [send_block(me, partner, hist_send.at[0])]
+    for off in range(1, half):
+        sends.append(send_block(me, lax.rem(me + 2 * off, n), hist_send.at[off]))
+    for copy in sends:
+        copy.start()
 
     relays = []
     for off in range(1, half):
@@ -170,16 +178,15 @@
     coeffs = basis.shape[1]
     flat = ztiles.reshape(rows, slots * tile, tile)
     hbm = pl.BlockSpec(memory_space=pltpu.HBM)
-    smem = pl.BlockSpec(memory_space=pltpu.SMEM)
     vmem = pl.BlockSpec(memory_space=pltpu.VMEM)
     bf16, f32 = jnp.bfloat16, jnp.float32
     dma = pltpu.SemaphoreType.DMA
     tiles = coeffs // LANES
     return pl.pallas_call(
         functools.partial(march_kernel, n),
-        out_shape=(jax.ShapeDtypeStruct((steps, dirs, width), bf16),
-                   jax.ShapeDtypeStruct((steps, dirs, coeffs // n), f32)),
-        in_specs=[hbm] * 5 + [smem] * 3,
+        out_shape=(pltpu.VMEM((steps, dirs, width), bf16),
+                   pltpu.VMEM((steps, dirs, coeffs // n), f32)),
+        in_specs=[hbm] * 8,
         out_specs=(vmem, vmem),
         scratch_shapes=[
             pltpu.VMEM((n * levels * rows + 1, dirs, LANES), bf16),
@@ -187,19 +194,23 @@
             pltpu.VMEM(zinv.shape, bf16),
             pltpu.VMEM(basis.shape, bf16),
             pltpu.VMEM(incident.shape, bf16),
+            pltpu.SMEM(columns.shape, jnp.int32),
+            pltpu.SMEM(lags.shape, jnp.int32),
+            pltpu.SMEM(counts.shape, jnp.int32),
             pltpu.VMEM((rows, 2 * dirs, slots * tile), bf16),
             pltpu.VMEM((rows, dirs, slots * tile), bf16),
             pltpu.VMEM((n * rows + 1, dirs, LANES), bf16),
             pltpu.VMEM((steps, tiles, dirs, LANES), f32),
             pltpu.VMEM((steps, n, dirs, LANES), f32),
-            dma((5,)), dma((levels * rows,)),
+            dma((7,)), dma((levels * rows,)),
             dma((n,)), dma((n,)), dma((n,)),
             dma((n,)), dma((n,)),
             dma((steps, n)), dma((steps, n)),
         ],
         compiler_params=pltpu.CompilerParams(
-            collective_id=0, has_side_effects=True, vmem_limit_bytes=67043328),
-    )(history, incident, flat, zinv, basis, columns, lags, counts)
+            collective_id=0, has_side_effects=True, vmem_limit_bytes=32 * 1024 * 1024),
+    )(*(pltpu.with_memory_space_constraint(x, pltpu.HBM)
+        for x in (history, incident, flat, zinv, basis, columns, lags, counts)))
 
 
 def solution(mesh):

time: 29.9 us -> 27.2 us (0.910)
  local copies, waits for them, and re-layouts: 2.6 us -> 1.2 us
  Pallas kernels: 26.3 us -> 25.2 us
    unnamed x2, local copies, waits for them, and re-layouts: 2.6 us -> 1.2 us
    pallas_call x1, Pallas kernels: 26.3 us -> 25.2 us  [on_device(): pl.pallas_call(functools.partial(march_kernel, n), out_shape=(pltpu.VMEM(...]
where the time goes in v3:
time: 27.2 us; the launch traced here: 27.1 us
  Pallas kernels  25.2 us (93%)
  local copies, waits for them, and re-layouts  1.2 us (4%)
  between operations  0.64 us (2%)
    pallas_call x1, Pallas kernels, on_device(): pl.pallas_call(functools.partial(march_kernel, n), out_shape=(pltpu.VMEM(...  25.2 us
    unnamed x2, local copies, waits for them, and re-layouts  1.2 us

profile of v3, /device:TPU:0, one launch (start us, length us, event | category | flops | bytes accessed | tf_op | source)
XLA Modules:
  0.0 27.1 jit_solution(11306186216354661725)
XLA Ops:
  0.6 25.2 %shard_map.95 = (bf16[2,8,384]{2,1,0:T(8,128)(2,1)S(1)}, f32[2,8,32]{2,1,0:T(8,128)S(1)}) custom-call(bf16[8,8,384]{2,1,0:T(8,128)(2,1)} %hist_hbm.1, bf16[2,8,384]{2,1,0:T(8,128)(2,1)} %inc_hbm.1, bf16[3,4096,128]{2,1,0:T(8,128)(2,1)} %bitcast.1, bf16[3,128,128]{2,1,0:T(8,128)(2,1)} %zinv_hbm.1, bf16[384,256]{1,0:T(8,128)(2,1)} %basis_hbm.1, ...), custom_call_target="tpu_custom_call" | custom-call | tf_op jit(solution)/shard_map/pallas_call | solution.py:185
  25.9 0.6 %copy.12 = bf16[2,8,384]{2,1,0:T(8,128)(2,1)} copy(bf16[2,8,384]{2,1,0:T(8,128)(2,1)S(1)} %get-tuple-element.2) | data formatting | bytes 24576
  26.5 0.6 %copy.13 = f32[2,8,32]{2,1,0:T(8,128)} copy(f32[2,8,32]{2,1,0:T(8,128)S(1)} %get-tuple-element.3) | data formatting | bytes 4096
